TPU v7x, 128 devices: a whole 4x4x4 slice. The times are simulated.
128 devices in a mesh: tm: 16 (over x, y_lo, core), space: 8 (over z, y_hi).
Axes of the slice: x: 4, y: 4 (y_hi: 2, y_lo: 2; y = y_hi * 2 + y_lo), z: 4, core: 2. Of those that a mesh axis runs over, the one named last changes fastest.
Arguments:
- input_field: float32 [64, 32, 32, 1024], P('tm', None, 'space'), may hold values from -6 to 6
- cotangent: float32 [64, 32, 32, 1024], P('tm', None, 'space'), may hold values from -6 to 6
- spectral_weights: float32 [2, 2, 16, 32, 32], replicated, may hold values from -0.75 to 0.75
- conv_kernel: float32 [2, 3, 32, 32], replicated, may hold values from -0.625 to 0.625
- mode_list: int32 [16], replicated, may hold values from 0 to 31, as said below
Outputs:
- grad_input: float32 [64, 32, 32, 1024], P('tm', None, 'space')
- grad_spectral: float32 [2, 2, 16, 32, 32], P(None, None, 'tm')
- grad_kernel: float32 [2, 3, 32, 32], replicated
Inputs may be any that keep to these rules, and one draw needn't show every extreme that they name: `mode_list`: 16 distinct frequencies in ascending order, with 0 and 31 among them.
All inputs are finite; a program needn't handle non-finite values.
Results may differ from a plain program's by a relative error of at most 0.00014.
Values sent between devices are 32-bit elements; how exact they have to be, the bound alone decides.
No kernel may reach another device: no remote copies, remote signals or barrier semaphores. Data moves between devices by JAX's collectives and lax.ppermute only.
A program may use at most 128 MiB of HBM per device.

v0:
```python
import math
import jax
import jax.numpy as jnp
from jax import lax
from jax.sharding import PartitionSpec as P

HIGHEST = lax.Precision.HIGHEST


def extended(value, sides, width):
    for axis, dim in sides:
        size, length = (lax.axis_size(axis), value.shape[dim])
        up = [(i, (i + 1) % size) for i in range(size - 1)]
        down = [(j, i) for i, j in up]
        last = lax.slice_in_dim(value, length - width, length, axis=dim)
        initial = lax.slice_in_dim(value, 0, width, axis=dim)
        before = lax.ppermute(last, axis, up)
        after = lax.ppermute(initial, axis, down)
        value = jnp.concatenate([before, value, after], axis=dim)
    return value


def tables(mode_list, time_count, total_time):
    time_steps = jnp.arange(time_count, dtype=jnp.int32)
    phase_index = mode_list[:, None] * time_steps[None, :] % total_time
    angles = phase_index.astype(jnp.float32) * (2.0 * math.pi / total_time)
    return (jnp.cos(angles), jnp.sin(angles))


def forward_dft(cosine_table, sine_table, flattened):
    time_count = flattened.shape[0]
    rows = flattened.reshape(time_count, -1)
    cosine_part = jnp.dot(cosine_table, rows, precision=HIGHEST)
    sine_part = -jnp.dot(sine_table, rows, precision=HIGHEST)
    stacked = jnp.stack([cosine_part, sine_part], axis=1)
    return stacked.reshape(cosine_table.shape[0], 2, flattened.shape[1], flattened.shape[2])


def inverse_dft(cosine_table, sine_table, coefficients, factor):
    mode_count = coefficients.shape[0]
    cosine_term = jnp.dot(
        cosine_table.T, coefficients[:, 0].reshape(mode_count, -1), precision=HIGHEST
    )
    sine_term = jnp.dot(sine_table.T, coefficients[:, 1].reshape(mode_count, -1), precision=HIGHEST)
    result = factor * (cosine_term - sine_term)
    return result.reshape(cosine_table.shape[1], coefficients.shape[2], coefficients.shape[3])


def mode_product(values, weight):
    return jnp.einsum("mcn,mcd->mdn", values, weight, precision=HIGHEST)


def mode_adjoint(values, weight):
    return jnp.einsum("mdn,mcd->mcn", values, weight, precision=HIGHEST)


def mode_outer(left_values, right_values):
    return jnp.einsum("mcn,mdn->mcd", left_values, right_values, precision=HIGHEST)


def channel_mix(coefficients, weight):
    real_part = mode_product(coefficients[:, 0], weight[0]) - mode_product(
        coefficients[:, 1], weight[1]
    )
    imag_part = mode_product(coefficients[:, 1], weight[0]) + mode_product(
        coefficients[:, 0], weight[1]
    )
    return jnp.stack([real_part, imag_part], axis=1)


def channel_mix_adjoint(sens_modes, weight):
    real_part = mode_adjoint(sens_modes[:, 0], weight[0]) + mode_adjoint(
        sens_modes[:, 1], weight[1]
    )
    imag_part = mode_adjoint(sens_modes[:, 1], weight[0]) - mode_adjoint(
        sens_modes[:, 0], weight[1]
    )
    return jnp.stack([real_part, imag_part], axis=1)


def weight_grad(coefficients, sens_modes):
    real_part = mode_outer(coefficients[:, 0], sens_modes[:, 0]) + mode_outer(
        coefficients[:, 1], sens_modes[:, 1]
    )
    imag_part = mode_outer(coefficients[:, 0], sens_modes[:, 1]) - mode_outer(
        coefficients[:, 1], sens_modes[:, 0]
    )
    return jnp.stack([real_part, imag_part], axis=0)


def convolve(padded, kernel, cells_x):
    result = jnp.einsum("tcxs,cd->tdxs", padded[:, :, 0:cells_x], kernel[0], precision=HIGHEST)
    for offset in range(1, 3):
        result = result + jnp.einsum(
            "tcxs,cd->tdxs",
            padded[:, :, offset : offset + cells_x],
            kernel[offset],
            precision=HIGHEST,
        )
    return result


def convolve_adjoint(sens_padded, kernel, cells_x):
    result = jnp.einsum(
        "tdxs,cd->tcxs", sens_padded[:, :, 2 : 2 + cells_x], kernel[0], precision=HIGHEST
    )
    for offset in range(1, 3):
        result = result + jnp.einsum(
            "tdxs,cd->tcxs",
            sens_padded[:, :, 2 - offset : 2 - offset + cells_x],
            kernel[offset],
            precision=HIGHEST,
        )
    return result


def gelu_exact(values):
    return jax.nn.gelu(values, approximate=False)


def on_device(input_field, cotangent, spectral_weights, conv_kernel, mode_list):
    groups = lax.axis_size("tm")
    total_time = input_field.shape[0] * groups
    layers = conv_kernel.shape[0]
    factor = 2.0 / total_time
    cosine_all, sine_all = tables(mode_list, total_time, total_time)
    state_field, gradient = (input_field, cotangent)
    time_local, channels, cells_x, cells_s = state_field.shape
    cell_count = cells_x * cells_s
    saved = []
    for layer_number in range(layers):
        padded = extended(state_field, (("space", 2),), 1)
        convolved = convolve(padded, conv_kernel[layer_number], cells_x)
        flattened = state_field.reshape(time_local, channels, cell_count)
        series_field = lax.all_to_all(flattened, "tm", split_axis=2, concat_axis=0, tiled=True)
        coefficients = forward_dft(cosine_all, sine_all, series_field)
        mixed = channel_mix(coefficients, spectral_weights[layer_number])
        returned = inverse_dft(cosine_all, sine_all, mixed, factor)
        spectral_part = lax.all_to_all(returned, "tm", split_axis=0, concat_axis=2, tiled=True)
        preact = spectral_part.reshape(state_field.shape) + convolved
        saved.append((padded, coefficients, preact))
        state_field = gelu_exact(preact)
    kernel_pieces = []
    mode_pieces = []
    for layer_number in reversed(range(layers)):
        padded, coefficients, preact = saved[layer_number]
        pullback = jax.vjp(gelu_exact, preact)[1]
        sensitivity = pullback(gradient)[0]
        kernel_piece = jnp.stack(
            [
                jnp.einsum(
                    "tcxs,tdxs->cd",
                    padded[:, :, offset : offset + cells_x],
                    sensitivity,
                    precision=HIGHEST,
                )
                for offset in range(3)
            ]
        )
        sens_padded = extended(sensitivity, (("space", 2),), 1)
        back_conv = convolve_adjoint(sens_padded, conv_kernel[layer_number], cells_x)
        flat_sens = sensitivity.reshape(time_local, channels, cell_count)
        series_sens = lax.all_to_all(flat_sens, "tm", split_axis=2, concat_axis=0, tiled=True)
        sens_modes = factor * forward_dft(cosine_all, sine_all, series_sens)
        mode_piece = weight_grad(coefficients, sens_modes)
        adjoint = channel_mix_adjoint(sens_modes, spectral_weights[layer_number])
        returned = inverse_dft(cosine_all, sine_all, adjoint, 1.0)
        back_spec = lax.all_to_all(returned, "tm", split_axis=0, concat_axis=2, tiled=True)
        gradient = back_spec.reshape(sensitivity.shape) + back_conv
        kernel_pieces.append(kernel_piece)
        mode_pieces.append(mode_piece)
    kernel_total = lax.psum(jnp.stack(kernel_pieces[::-1]), ("tm", "space"))
    mode_stack = lax.psum_scatter(
        jnp.stack(mode_pieces[::-1]), "tm", scatter_dimension=2, tiled=True
    )
    mode_total = lax.psum(mode_stack, "space")
    return (gradient, mode_total, kernel_total)


def solution(mesh):
    placed = (P("tm", None, "space", None), P("tm", None, "space", None), P(), P(), P())
    return jax.shard_map(
        on_device,
        mesh=mesh,
        in_specs=placed,
        out_specs=(P("tm", None, "space", None), P(None, None, "tm", None, None), P()),
        check_vma=False,
    )
```

profile of v0, /device:TPU:0, one launch (start us, length us, event | category | flops | bytes accessed | tf_op | source)
XLA Modules:
  0.0 852.2 jit_solution(5890445966441035744)
XLA Ops:
  7.2 7.8 copy.219
  14.9 8.5 reshape.161
  23.4 33.1 %all_to_all.120 = f32[16,1,32768]{2,1,0:T(1,128)} all-to-all(f32[16,1,32768]{2,1,0:T(1,128)S(1)} %reshape.161), channel_id=1, replica_groups=mesh['tm'=16,'space'=8] {'tm'}, dimensions={0} | all-to-all | bytes 4194304 | tf_op jit(solution)/shard_map/all_to_all | solution.py:135
  57.0 7.3 reduce
  70.7 6.9 copy.330
  108.9 23.0 %collective-permute-done = f32[4,32,1,1024]{3,1,2,0:T(8,128)S(1)} collective-permute-done((f32[4,32,1,1024]{3,1,2,0:T(8,128)S(1)}, f32[4,32,1,1024]{3,1,2,0:T(8,128)S(1)}, u32[]{:S(2)}, u32[]{:S(2)}) %collective-permute-start) | collective-permute-done | bytes 524320 | tf_op jit(solution)/shard_map/ppermute | solution.py:17
  134.9 11.6 %collective-permute-done.1 = f32[4,32,1,1024]{3,1,2,0:T(8,128)S(1)} collective-permute-done((f32[4,32,1,1024]{3,1,2,0:T(8,128)S(1)}, f32[4,32,1,1024]{3,1,2,0:T(8,128)S(1)}, u32[]{:S(2)}, u32[]{:S(2)}) %collective-permute-start.1) | collective-permute-done | bytes 524320 | tf_op jit(solution)/shard_map/ppermute | solution.py:18
  155.9 10.0 %multiply_multiply_fusion.10 = (f32[4,32,4,1024]{3,1,2,0:T(8,128)S(1)}, f32[4,32,4,1024]{3,1,2,0:T(8,128)}) fusion(f32[4,32,5,1024]{3,1,2,0:T(8,128)} %constant_dynamic-update-slice_fusion.2, f32[2,3,32,32]{3,2,1,0:T(8,128)S(1)} %copy-done.28, f32[32,4,4,1024]{3,0,2,1:T(8,128)} %fusion.154, f32[4,4,1024,32]{2,3,1,0:T(8,128)} %fusion.157, ...), kind=kOutput, calls=%fused_computation.86 | convolution fusion | flops 236453888 | bytes 13123584 | tf_op jit(solution)/shard_map/tcxs,cd->tdxs/dot_general | solution.py:94
  171.8 9.5 %reshape.163 = f32[16,1,32768]{2,1,0:T(1,128)} reshape(f32[4096,4,32]{2,1,0:T(4,128)} %bitcast.414) | data formatting | bytes 4194304
  181.3 32.7 %all_to_all.121 = f32[16,1,32768]{2,1,0:T(1,128)} all-to-all(f32[16,1,32768]{2,1,0:T(1,128)} %reshape.163), channel_id=1, replica_groups=mesh['tm'=16,'space'=8] {'tm'}, dimensions={0} | all-to-all | bytes 4194304 | tf_op jit(solution)/shard_map/all_to_all | solution.py:135
  214.0 8.6 %reduce.1 = f32[16,32768]{1,0:T(8,128)} reduce(f32[16,1,32768]{2,1,0:T(1,128)} %all_to_all.121, f32[]{:T(128)} %broadcast.353), dimensions={1}, to_apply=%all_to_all.94.reduce_sub_computation | reduce | bytes 4194308 | tf_op jit(solution)/shard_map/all_to_all | solution.py:135
  222.6 7.7 reshape.164
  230.3 8.4 copy.239
  270.5 23.8 %collective-permute-done.2 = f32[4,32,1,1024]{3,1,2,0:T(8,128)S(1)} collective-permute-done((f32[4,32,1,1024]{3,1,2,0:T(8,128)S(1)}, f32[4,32,1,1024]{3,1,2,0:T(8,128)S(1)}, u32[]{:S(2)}, u32[]{:S(2)}) %collective-permute-start.2) | collective-permute-done | bytes 524320 | tf_op jit(solution)/shard_map/ppermute | solution.py:17
  309.3 10.8 %fusion.26 = f32[4,32,4,1024]{3,1,2,0:T(8,128)} fusion(f32[4,32,4,1024]{3,2,1,0:T(4,128)} %param.6, f32[4,4,1024,32]{2,3,1,0:T(8,128)} %fusion.20, f32[4,4,1024,32]{2,3,1,0:T(8,128)} %fusion.142, f32[4,32,4,1024]{3,2,1,0:T(4,128)} %reshape.128, f32[4,32,1,1024]{3,1,2,0:T(8,128)} %collective-permute-done.3, f32[4,32,4,1024]{3,1,2,0:T(8,128)S(1)} %get-tuple-element.29, ...), kind=kOutput, calls=%fused_computation.38 | convolution fusion | flops 240779264 | bytes 13123584 | tf_op jit(solution)/shard_map/tcxs,cd->tdxs/dot_general | solution.py:94
  320.1 7.8 copy.332
  328.0 9.5 %reshape.165 = f32[16,1,32768]{2,1,0:T(1,128)} reshape(f32[4096,4,32]{2,1,0:T(4,128)} %bitcast.415) | data formatting | bytes 4194304
  337.5 32.9 %all_to_all.122 = f32[16,1,32768]{2,1,0:T(1,128)} all-to-all(f32[16,1,32768]{2,1,0:T(1,128)} %reshape.165), channel_id=1, replica_groups=mesh['tm'=16,'space'=8] {'tm'}, dimensions={0} | all-to-all | bytes 4194304 | tf_op jit(solution)/shard_map/all_to_all | solution.py:163
  370.4 8.6 %reduce.2 = f32[16,32768]{1,0:T(8,128)} reduce(f32[16,1,32768]{2,1,0:T(1,128)} %all_to_all.122, f32[]{:T(128)} %broadcast.353), dimensions={1}, to_apply=%all_to_all.100.reduce_sub_computation | reduce | bytes 4194308 | tf_op jit(solution)/shard_map/all_to_all | solution.py:163
  379.0 7.7 reshape.166
  386.7 8.4 copy.254
  421.4 6.8 collective-permute-start.5
  438.2 17.2 %collective-permute-done.4 = f32[4,32,1,1024]{3,1,2,0:T(8,128)S(1)} collective-permute-done((f32[4,32,1,1024]{3,1,2,0:T(8,128)S(1)}, f32[4,32,1,1024]{3,1,2,0:T(8,128)S(1)}, u32[]{:S(2)}, u32[]{:S(2)}) %collective-permute-start.4) | collective-permute-done | bytes 524320 | tf_op jit(solution)/shard_map/ppermute | solution.py:18
  464.0 9.6 %multiply_add_fusion = f32[4,32,4,1024]{3,1,2,0:T(8,128)S(1)} fusion(f32[4,32,4,1024]{3,2,1,0:T(4,128)} %reshape.133, f32[4,4,1024,32]{2,3,1,0:T(8,128)} %fusion.2, f32[4,4,1024,32]{2,3,1,0:T(8,128)} %fusion.140, f32[4,32,4,1024]{3,1,2,0:T(8,128)} %get-tuple-element.30, f32[4,32,4,1024]{3,1,2,0:T(8,128)} %fusion.26, ...), kind=kOutput, calls=%fused_computation.57 | convolution fusion | flops 240779264 | bytes 13123584 | tf_op jit(solution)/shard_map/tdxs,cd->tcxs/dot_general | solution.py:108
  479.6 9.5 %reshape.167 = f32[16,1,32768]{2,1,0:T(1,128)} reshape(f32[4096,4,32]{2,1,0:T(4,128)} %bitcast.416) | data formatting | bytes 4194304
  504.0 7.3 collective-permute-start.7
  522.0 8.6 %reduce.3 = f32[16,32768]{1,0:T(8,128)} reduce(f32[16,1,32768]{2,1,0:T(1,128)} %all-to-all-done.6, f32[]{:T(128)} %broadcast.353), dimensions={1}, to_apply=%all_to_all.106.reduce_sub_computation | reduce | bytes 4194308 | tf_op jit(solution)/shard_map/all_to_all | solution.py:163
  530.6 7.7 reshape.168
  538.3 8.1 copy.272
  569.6 88.0 %psum.15 = f32[2,3,32,32]{3,2,1,0:T(8,128)} all-reduce(f32[2,3,32,32]{3,2,1,0:T(8,128)S(1)} %pad_maximum_fusion.11), channel_id=1, replica_groups=mesh['tm'=16,'space'=8] {'tm','space'}, use_global_device_ids=true, to_apply=%region_2.3 | all-reduce | flops 6144 | bytes 49152 | tf_op jit(solution)/shard_map/psum | solution.py:172
  671.1 112.7 %all-reduce.3.cloned.1.call-done = f32[2,2,16,32,32]{4,3,2,1,0:T(8,128)} async-done(((f32[2,2,16,32,32]{4,3,2,1,0:T(8,128)}), f32[2,2,16,32,32]{4,3,2,1,0:T(8,128)}) %all-reduce.3.cloned.1.call-update) | async-done | bytes 262160
  785.1 43.4 %psum.14 = f32[2,2,1,32,32]{4,3,2,1,0:T(8,128)} all-reduce(f32[2,2,1,32,32]{4,3,2,1,0:T(8,128)S(1)} %constant_dynamic-slice_fusion), channel_id=1, replica_groups=mesh['tm'=16,'space'=8] {'space'}, use_global_device_ids=true, to_apply=%region_1.2 | all-reduce | flops 4096 | bytes 32768 | tf_op jit(solution)/shard_map/psum | solution.py:176
  (198 shorter events, 233.0 us)
Async XLA Ops:
  81.2 5.9 copy-start.11
  92.8 4.6 copy-start.1
  92.8 58.0 %all-to-all-start.1 = ((f32[64,32,256]{2,1,0:T(8,128)}), f32[64,32,256]{2,1,0:T(8,128)}, u32[]{:S(2)}, u32[]{:S(2)}) async-start(f32[64,32,256]{2,1,0:T(8,128)} %bitcast.439), calls=%async_computation.1 | async-start | bytes 4194304 | tf_op jit(solution)/shard_map/all_to_all | solution.py:139
  97.4 7.2 copy-start.28
  98.3 33.6 %collective-permute-start = (f32[4,32,1,1024]{3,1,2,0:T(8,128)S(1)}, f32[4,32,1,1024]{3,1,2,0:T(8,128)S(1)}, u32[]{:S(2)}, u32[]{:S(2)}) collective-permute-start(f32[4,32,1,1024]{3,1,2,0:T(8,128)S(1)} %copy.463), channel_id=1, source_target_pairs={{0,1},{1,2},{2,3},{3,4},{4,5},{5,6},{6,7},{8,9},{9,10},{10,11},{11... | collective-permute-start | bytes 1572872 | tf_op jit(solution)/shard_map/ppermute | solution.py:17
  103.2 43.2 %collective-permute-start.1 = (f32[4,32,1,1024]{3,1,2,0:T(8,128)S(1)}, f32[4,32,1,1024]{3,1,2,0:T(8,128)S(1)}, u32[]{:S(2)}, u32[]{:S(2)}) collective-permute-start(f32[4,32,1,1024]{3,1,2,0:T(8,128)S(1)} %copy.464), channel_id=1, source_target_pairs={{1,0},{2,1},{3,2},{4,3},{5,4},{6,5},{7,6},{9,8},{10,9},{11,10},{12... | collective-permute-start | bytes 1572872 | tf_op jit(solution)/shard_map/ppermute | solution.py:18
  134.9 12.5 %copy-start.23 = (f32[4,32,5,1024]{3,1,2,0:T(8,128)}, f32[4,32,5,1024]{3,1,2,0:T(8,128)S(1)}, u32[]{:S(2)}) copy-start(f32[4,32,5,1024]{3,1,2,0:T(8,128)S(1)} %get-tuple-element.24) | copy-start | bytes 7864324
  238.7 4.0 copy-start.3
  242.7 7.1 copy-start.13
  255.3 43.1 %all-to-all-start.3 = ((f32[64,32,256]{2,1,0:T(8,128)}), f32[64,32,256]{2,1,0:T(8,128)}, u32[]{:S(2)}, u32[]{:S(2)}) async-start(f32[64,32,256]{2,1,0:T(8,128)} %bitcast.440), calls=%async_computation.3 | async-start | bytes 4194304 | tf_op jit(solution)/shard_map/all_to_all | solution.py:139
  260.7 33.6 %collective-permute-start.2 = (f32[4,32,1,1024]{3,1,2,0:T(8,128)S(1)}, f32[4,32,1,1024]{3,1,2,0:T(8,128)S(1)}, u32[]{:S(2)}, u32[]{:S(2)}) collective-permute-start(f32[4,32,1,1024]{3,1,2,0:T(8,128)S(1)} %get-tuple-element.20), channel_id=1, source_target_pairs={{0,1},{1,2},{2,3},{3,4},{4,5},{5,6},{6,7},{8,9},{9,10},{10,11},{11... | collective-permute-start | bytes 1572872 | tf_op jit(solution)/shard_map/ppermute | solution.py:17
  265.8 43.5 %collective-permute-start.3 = (f32[4,32,1,1024]{3,1,2,0:T(8,128)}, f32[4,32,1,1024]{3,1,2,0:T(8,128)}, u32[]{:S(2)}, u32[]{:S(2)}) collective-permute-start(f32[4,32,1,1024]{3,1,2,0:T(8,128)} %get-tuple-element.19), channel_id=1, source_target_pairs={{1,0},{2,1},{3,2},{4,3},{5,4},{6,5},{7,6},{9,8},{10,9},{11,10},{12... | collective-permute-start | bytes 1572872 | tf_op jit(solution)/shard_map/ppermute | solution.py:18
  402.2 5.1 copy-start.17
  412.7 4.6 copy-start.32
  412.7 46.2 %all-to-all-start.5 = ((f32[64,32,256]{2,1,0:T(8,128)}), f32[64,32,256]{2,1,0:T(8,128)}, u32[]{:S(2)}, u32[]{:S(2)}) async-start(f32[64,32,256]{2,1,0:T(8,128)} %bitcast.438), calls=%async_computation.5 | async-start | bytes 4194304 | tf_op jit(solution)/shard_map/all_to_all | solution.py:168
  417.3 10.9 %copy-start = (f32[4,32,4,1024]{3,1,2,0:T(8,128)S(1)}, f32[4,32,4,1024]{3,1,2,0:T(8,128)}, u32[]{:S(2)}) copy-start(f32[4,32,4,1024]{3,1,2,0:T(8,128)} %fusion.26) | copy-start | bytes 6291460
  420.1 35.4 %collective-permute-start.4 = (f32[4,32,1,1024]{3,1,2,0:T(8,128)S(1)}, f32[4,32,1,1024]{3,1,2,0:T(8,128)S(1)}, u32[]{:S(2)}, u32[]{:S(2)}) collective-permute-start(f32[4,32,1,1024]{3,1,2,0:T(8,128)S(1)} %get-tuple-element.18), channel_id=1, source_target_pairs={{1,0},{2,1},{3,2},{4,3},{5,4},{6,5},{7,6},{9,8},{10,9},{11,10},{12... | collective-permute-start | bytes 1572872 | tf_op jit(solution)/shard_map/ppermute | solution.py:18
  421.4 42.6 %collective-permute-start.5 = (f32[4,32,1,1024]{3,1,2,0:T(8,128)}, f32[4,32,1,1024]{3,1,2,0:T(8,128)}, u32[]{:S(2)}, u32[]{:S(2)}) collective-permute-start(f32[4,32,1,1024]{3,1,2,0:T(8,128)} %get-tuple-element.17), channel_id=1, source_target_pairs={{0,1},{1,2},{2,3},{3,4},{4,5},{5,6},{6,7},{8,9},{9,10},{10,11},{11... | collective-permute-start | bytes 1572872 | tf_op jit(solution)/shard_map/ppermute | solution.py:17
  489.0 33.0 %all-to-all-start.6 = ((f32[16,1,32768]{2,1,0:T(1,128)}), f32[16,1,32768]{2,1,0:T(1,128)}, u32[]{:S(2)}, u32[]{:S(2)}) async-start(f32[16,1,32768]{2,1,0:T(1,128)} %reshape.167), calls=%async_computation.6 | async-start | bytes 4194304 | tf_op jit(solution)/shard_map/all_to_all | solution.py:163
  494.2 4.6 copy-start.14
  494.2 4.6 copy-start.18
  494.2 5.8 copy-start.10
  494.2 5.8 copy-start.16
  500.1 11.2 %copy-start.2 = (f32[4,32,4,1024]{3,2,1,0:T(4,128)S(1)}, f32[4,32,4,1024]{3,2,1,0:T(4,128)}, u32[]{:S(2)}) copy-start(f32[4,32,4,1024]{3,2,1,0:T(4,128)} %param.5) | copy-start | bytes 6291460
  502.7 163.9 %collective-permute-start.6 = (f32[4,32,1,1024]{3,1,2,0:T(8,128)}, f32[4,32,1,1024]{3,1,2,0:T(8,128)}, u32[]{:S(2)}, u32[]{:S(2)}) collective-permute-start(f32[4,32,1,1024]{3,1,2,0:T(8,128)} %get-tuple-element.16), channel_id=1, source_target_pairs={{1,0},{2,1},{3,2},{4,3},{5,4},{6,5},{7,6},{9,8},{10,9},{11,10},{12... | collective-permute-start | bytes 1572872 | tf_op jit(solution)/shard_map/ppermute | solution.py:18
  504.0 331.9 %collective-permute-start.7 = (f32[4,32,1,1024]{3,1,2,0:T(8,128)}, f32[4,32,1,1024]{3,1,2,0:T(8,128)}, u32[]{:S(2)}, u32[]{:S(2)}) collective-permute-start(f32[4,32,1,1024]{3,1,2,0:T(8,128)} %get-tuple-element.15), channel_id=1, source_target_pairs={{0,1},{1,2},{2,3},{3,4},{4,5},{5,6},{6,7},{8,9},{9,10},{10,11},{11... | collective-permute-start | bytes 1572872 | tf_op jit(solution)/shard_map/ppermute | solution.py:17
  514.1 3.6 copy-start.24
  553.6 5.1 copy-start.21
  564.1 5.4 copy-start.29
  564.1 264.4 %all-to-all-start.7 = ((f32[64,32,256]{2,1,0:T(8,128)}), f32[64,32,256]{2,1,0:T(8,128)}, u32[]{:S(2)}, u32[]{:S(2)}) async-start(f32[64,32,256]{2,1,0:T(8,128)} %bitcast.437), calls=%async_computation.7 | async-start | bytes 4194304 | tf_op jit(solution)/shard_map/all_to_all | solution.py:168
  569.5 214.2 %all-reduce.3.cloned.1.call-start = ((), (), s32[]{:S(2)}) async-start(), calls=%async_computation.8 | async-start | bytes 2097152
  657.6 4.7 copy-start.22
  (15 other events, 35.9 us)
Sparse Core Ops, SparseCore 0:
  666.7 117.0 all-reduce.2
where the time goes:
time: 862 us; the launch traced here: 852 us
  blocking collectives  230 us (27%)
  waiting for transfers between devices  194 us (23%)
  local copies, waits for them, and re-layouts  186 us (22%)
  matrix products  138 us (16%)
  starting transfers between devices  53.3 us (6%)
  other arithmetic  35.2 us (4%)
  between operations  15.6 us (2%)
    unnamed x2, waiting for transfers between devices  113 us
    unnamed x102, local copies, waits for them, and re-layouts  103 us
    psum x1, blocking collectives, on_device(): kernel_total = lax.psum(jnp.stack(kernel_pieces[::-1]), ('tm', 'space'))  88 us
    all_to_all x2, blocking collectives, on_device(): lax.all_to_all(flattened, 'tm', split_axis=2, concat_axis=0, tiled=True)  65.8 us
    ppermute x4, waiting for transfers between devices, extended(): before = lax.ppermute(last, axis, up)  46.8 us
    psum x1, blocking collectives, on_device(): mode_total = lax.psum(mode_stack, 'space')  43.4 us
    all_to_all x1, blocking collectives, on_device(): lax.all_to_all(flat_sens, 'tm', split_axis=2, concat_axis=0, tiled=True)  32.9 us
    ppermute x4, waiting for transfers between devices, extended(): after = lax.ppermute(initial, axis, down)  32.3 us
  transfers between devices with their start and end apart: 14, of which 7 were waited for; matrix products, arithmetic and copies ran while one was open for 15% of the time, Pallas kernels for 0%

commit v1 on v0

--- a/solution.py
+++ b/solution.py
@@ -169,7 +169,7 @@
         gradient = back_spec.reshape(sensitivity.shape) + back_conv
         kernel_pieces.append(kernel_piece)
         mode_pieces.append(mode_piece)
-    kernel_total = lax.psum(jnp.stack(kernel_pieces[::-1]), ("tm", "space"))
+    kernel_total = jnp.sum(lax.all_gather(jnp.stack(kernel_pieces[::-1]), ("tm", "space")), axis=0)
     mode_stack = lax.psum_scatter(
         jnp.stack(mode_pieces[::-1]), "tm", scatter_dimension=2, tiled=True
     )

time: 862 us -> 947 us (1.099)
  waiting for transfers between devices: 194 us -> 347 us
  blocking collectives: 230 us -> 142 us
    all_gather x0 -> x1, waiting for transfers between devices: none -> 151 us  [on_device(): lax.all_gather(jnp.stack(kernel_pieces[::-1]), ('tm', 'space'))]
    psum x1 -> x0, blocking collectives: 88 us -> none  [on_device(): kernel_total = lax.psum(jnp.stack(kernel_pieces[::-1]), ('tm', 'space'))]
    unnamed x2 -> x3, waiting for transfers between devices: 113 us -> 64.5 us
    ppermute x4, waiting for transfers between devices: 32.3 us -> 74.2 us  [extended(): after = lax.ppermute(initial, axis, down)]
    unnamed x102 -> x108, local copies, waits for them, and re-layouts: 103 us -> 104 us
  transfers between devices with their start and end apart: 14 -> 15, of which waited for: 7 -> 9; matrix products, arithmetic and copies ran while one was open for 15% -> 11% of each run, Pallas kernels for 0% -> 0%
where the time goes in v1:
time: 947 us; the launch traced here: 930 us
  waiting for transfers between devices  347 us (37%)
  local copies, waits for them, and re-layouts  187 us (20%)
  blocking collectives  142 us (15%)
  matrix products  141 us (15%)
  starting transfers between devices  53 us (6%)
  other arithmetic  42.2 us (4%)
  between operations  17.1 us (2%)
    all_gather x1, waiting for transfers between devices, on_device(): lax.all_gather(jnp.stack(kernel_pieces[::-1]), ('tm', 'space'))  151 us
    unnamed x108, local copies, waits for them, and re-layouts  104 us
    ppermute x4, waiting for transfers between devices, extended(): after = lax.ppermute(initial, axis, down)  74.2 us
    all_to_all x2, blocking collectives, on_device(): lax.all_to_all(flattened, 'tm', split_axis=2, concat_axis=0, tiled=True)  65.8 us
    unnamed x3, waiting for transfers between devices  64.5 us
    ppermute x4, waiting for transfers between devices, extended(): before = lax.ppermute(last, axis, up)  46.9 us
    psum x1, blocking collectives, on_device(): mode_total = lax.psum(mode_stack, 'space')  43.4 us
    all_to_all x1, blocking collectives, on_device(): lax.all_to_all(flat_sens, 'tm', split_axis=2, concat_axis=0, tiled=True)  32.9 us
  transfers between devices with their start and end apart: 15, of which 9 were waited for; matrix products, arithmetic and copies ran while one was open for 11% of the time, Pallas kernels for 0%

profile of v1, /device:TPU:0, one launch (start us, length us, event | category | flops | bytes accessed | tf_op | source)
XLA Modules:
  0.0 929.7 jit_solution(859945241219756764)
XLA Ops:
  8.0 7.8 copy.219
  15.8 8.5 reshape.162
  24.3 33.1 %all_to_all.120 = f32[16,1,32768]{2,1,0:T(1,128)} all-to-all(f32[16,1,32768]{2,1,0:T(1,128)S(1)} %reshape.162), channel_id=1, replica_groups=mesh['tm'=16,'space'=8] {'tm'}, dimensions={0} | all-to-all | bytes 4194304 | tf_op jit(solution)/shard_map/all_to_all | solution.py:135
  58.0 7.3 reduce
  109.8 23.0 %collective-permute-done = f32[4,32,1,1024]{3,1,2,0:T(8,128)S(1)} collective-permute-done((f32[4,32,1,1024]{3,1,2,0:T(8,128)S(1)}, f32[4,32,1,1024]{3,1,2,0:T(8,128)S(1)}, u32[]{:S(2)}, u32[]{:S(2)}) %collective-permute-start) | collective-permute-done | bytes 524320 | tf_op jit(solution)/shard_map/ppermute | solution.py:17
  135.8 11.6 %collective-permute-done.1 = f32[4,32,1,1024]{3,1,2,0:T(8,128)S(1)} collective-permute-done((f32[4,32,1,1024]{3,1,2,0:T(8,128)S(1)}, f32[4,32,1,1024]{3,1,2,0:T(8,128)S(1)}, u32[]{:S(2)}, u32[]{:S(2)}) %collective-permute-start.1) | collective-permute-done | bytes 524320 | tf_op jit(solution)/shard_map/ppermute | solution.py:18
  156.7 10.0 %multiply_multiply_fusion.10 = (f32[4,32,4,1024]{3,1,2,0:T(8,128)S(1)}, f32[4,32,4,1024]{3,1,2,0:T(8,128)}) fusion(f32[4,32,5,1024]{3,1,2,0:T(8,128)} %constant_dynamic-update-slice_fusion.2, f32[2,3,32,32]{3,2,1,0:T(8,128)S(1)} %copy-done.29, f32[32,4,4,1024]{3,0,2,1:T(8,128)} %fusion.154, f32[4,4,1024,32]{2,3,1,0:T(8,128)} %fusion.157, ...), kind=kOutput, calls=%fused_computation.86 | convolution fusion | flops 236453888 | bytes 13123584 | tf_op jit(solution)/shard_map/tcxs,cd->tdxs/dot_general | solution.py:94
  172.8 9.5 %reshape.164 = f32[16,1,32768]{2,1,0:T(1,128)} reshape(f32[4096,4,32]{2,1,0:T(4,128)} %bitcast.415) | data formatting | bytes 4194304
  182.3 32.7 %all_to_all.121 = f32[16,1,32768]{2,1,0:T(1,128)} all-to-all(f32[16,1,32768]{2,1,0:T(1,128)} %reshape.164), channel_id=1, replica_groups=mesh['tm'=16,'space'=8] {'tm'}, dimensions={0} | all-to-all | bytes 4194304 | tf_op jit(solution)/shard_map/all_to_all | solution.py:135
  215.1 8.6 reduce.1
  223.7 7.7 reshape.165
  231.4 8.4 copy.239
  271.6 23.9 %collective-permute-done.2 = f32[4,32,1,1024]{3,1,2,0:T(8,128)S(1)} collective-permute-done((f32[4,32,1,1024]{3,1,2,0:T(8,128)S(1)}, f32[4,32,1,1024]{3,1,2,0:T(8,128)S(1)}, u32[]{:S(2)}, u32[]{:S(2)}) %collective-permute-start.2) | collective-permute-done | bytes 524320 | tf_op jit(solution)/shard_map/ppermute | solution.py:17
  310.4 10.8 %fusion.26 = f32[4,32,4,1024]{3,1,2,0:T(8,128)} fusion(f32[4,32,4,1024]{3,2,1,0:T(4,128)} %param.6, f32[4,4,1024,32]{2,3,1,0:T(8,128)} %fusion.20, f32[4,4,1024,32]{2,3,1,0:T(8,128)} %fusion.142, f32[4,32,4,1024]{3,2,1,0:T(4,128)} %reshape.128, f32[4,32,1,1024]{3,1,2,0:T(8,128)} %collective-permute-done.3, f32[4,32,4,1024]{3,1,2,0:T(8,128)S(1)} %get-tuple-element.29, ...), kind=kOutput, calls=%fused_computation.38 | convolution fusion | flops 240779264 | bytes 13123584 | tf_op jit(solution)/shard_map/tcxs,cd->tdxs/dot_general | solution.py:94
  321.2 7.8 copy.332
  329.0 9.5 %reshape.166 = f32[16,1,32768]{2,1,0:T(1,128)} reshape(f32[4096,4,32]{2,1,0:T(4,128)} %bitcast.416) | data formatting | bytes 4194304
  338.4 32.9 %all_to_all.122 = f32[16,1,32768]{2,1,0:T(1,128)} all-to-all(f32[16,1,32768]{2,1,0:T(1,128)} %reshape.166), channel_id=1, replica_groups=mesh['tm'=16,'space'=8] {'tm'}, dimensions={0} | all-to-all | bytes 4194304 | tf_op jit(solution)/shard_map/all_to_all | solution.py:163
  371.4 8.6 reduce.2
  380.0 7.7 reshape.167
  387.6 8.4 copy.254
  434.8 21.5 %collective-permute-done.4 = f32[4,32,1,1024]{3,1,2,0:T(8,128)S(1)} collective-permute-done((f32[4,32,1,1024]{3,1,2,0:T(8,128)S(1)}, f32[4,32,1,1024]{3,1,2,0:T(8,128)S(1)}, u32[]{:S(2)}, u32[]{:S(2)}) %collective-permute-start.4) | collective-permute-done | bytes 524320 | tf_op jit(solution)/shard_map/ppermute | solution.py:18
  464.6 9.6 %multiply_add_fusion = f32[4,32,4,1024]{3,1,2,0:T(8,128)S(1)} fusion(f32[4,32,4,1024]{3,2,1,0:T(4,128)} %reshape.133, f32[4,4,1024,32]{2,3,1,0:T(8,128)} %fusion.2, f32[4,4,1024,32]{2,3,1,0:T(8,128)} %fusion.140, f32[4,32,4,1024]{3,1,2,0:T(8,128)} %get-tuple-element.30, f32[4,32,4,1024]{3,1,2,0:T(8,128)} %fusion.26, ...), kind=kOutput, calls=%fused_computation.57 | convolution fusion | flops 240779264 | bytes 13123584 | tf_op jit(solution)/shard_map/tdxs,cd->tcxs/dot_general | solution.py:108
  480.1 9.5 %reshape.168 = f32[16,1,32768]{2,1,0:T(1,128)} reshape(f32[4096,4,32]{2,1,0:T(4,128)} %bitcast.417) | data formatting | bytes 4194304
  512.5 10.0 %all-to-all-done.6 = f32[16,1,32768]{2,1,0:T(1,128)} async-done(((f32[16,1,32768]{2,1,0:T(1,128)}), f32[16,1,32768]{2,1,0:T(1,128)}, u32[]{:S(2)}, u32[]{:S(2)}) %all-to-all-start.6) | async-done | bytes 2097184 | tf_op jit(solution)/shard_map/all_to_all | solution.py:163
  522.5 9.0 reduce.3
  531.5 7.7 reshape.169
  539.2 8.1 copy.272
  586.3 7.1 collective-permute-start.7
  596.8 37.7 %collective-permute-done.6 = f32[4,32,1,1024]{3,1,2,0:T(8,128)S(1)} collective-permute-done((f32[4,32,1,1024]{3,1,2,0:T(8,128)}, f32[4,32,1,1024]{3,1,2,0:T(8,128)S(1)}, u32[]{:S(2)}, u32[]{:S(2)}) %collective-permute-start.6) | collective-permute-done | bytes 524320 | tf_op jit(solution)/shard_map/ppermute | solution.py:18
  637.9 64.5 %all-reduce.3.cloned.1.call-done = f32[2,2,16,32,32]{4,3,2,1,0:T(8,128)} async-done(((f32[2,2,16,32,32]{4,3,2,1,0:T(8,128)}), f32[2,2,16,32,32]{4,3,2,1,0:T(8,128)}) %all-reduce.3.cloned.1.call-update) | async-done | bytes 262160
  703.9 43.4 %psum.7 = f32[2,2,1,32,32]{4,3,2,1,0:T(8,128)} all-reduce(f32[2,2,1,32,32]{4,3,2,1,0:T(8,128)S(1)} %constant_dynamic-slice_fusion), channel_id=1, replica_groups=mesh['tm'=16,'space'=8] {'space'}, use_global_device_ids=true, to_apply=%region_1.2 | all-reduce | flops 4096 | bytes 32768 | tf_op jit(solution)/shard_map/psum | solution.py:176
  763.7 151.4 %all-gather.3.cloned.1.call-done = f32[256,3,32,32]{3,2,1,0:T(8,128)} async-done(((f32[2,3,32,32]{3,2,1,0:T(8,128)}), f32[256,3,32,32]{3,2,1,0:T(8,128)}) %all-gather.3.cloned.1.call-update) | async-done | bytes 3145744 | tf_op jit(solution)/shard_map/all_gather | solution.py:172
  (207 shorter events, 255.4 us)
Async XLA Ops:
  82.1 5.9 copy-start.13
  93.7 4.6 copy-start.4
  93.7 58.0 %all-to-all-start.1 = ((f32[64,32,256]{2,1,0:T(8,128)}), f32[64,32,256]{2,1,0:T(8,128)}, u32[]{:S(2)}, u32[]{:S(2)}) async-start(f32[64,32,256]{2,1,0:T(8,128)} %bitcast.440), calls=%async_computation.1 | async-start | bytes 4194304 | tf_op jit(solution)/shard_map/all_to_all | solution.py:139
  98.3 7.2 copy-start.29
  99.2 33.6 %collective-permute-start = (f32[4,32,1,1024]{3,1,2,0:T(8,128)S(1)}, f32[4,32,1,1024]{3,1,2,0:T(8,128)S(1)}, u32[]{:S(2)}, u32[]{:S(2)}) collective-permute-start(f32[4,32,1,1024]{3,1,2,0:T(8,128)S(1)} %copy.463), channel_id=1, source_target_pairs={{0,1},{1,2},{2,3},{3,4},{4,5},{5,6},{6,7},{8,9},{9,10},{10,11},{11... | collective-permute-start | bytes 1572872 | tf_op jit(solution)/shard_map/ppermute | solution.py:17
  104.2 43.2 %collective-permute-start.1 = (f32[4,32,1,1024]{3,1,2,0:T(8,128)S(1)}, f32[4,32,1,1024]{3,1,2,0:T(8,128)S(1)}, u32[]{:S(2)}, u32[]{:S(2)}) collective-permute-start(f32[4,32,1,1024]{3,1,2,0:T(8,128)S(1)} %copy.464), channel_id=1, source_target_pairs={{1,0},{2,1},{3,2},{4,3},{5,4},{6,5},{7,6},{9,8},{10,9},{11,10},{12... | collective-permute-start | bytes 1572872 | tf_op jit(solution)/shard_map/ppermute | solution.py:18
  135.8 12.5 %copy-start.25 = (f32[4,32,5,1024]{3,1,2,0:T(8,128)}, f32[4,32,5,1024]{3,1,2,0:T(8,128)S(1)}, u32[]{:S(2)}) copy-start(f32[4,32,5,1024]{3,1,2,0:T(8,128)S(1)} %get-tuple-element.24) | copy-start | bytes 7864324
  166.7 265.3 %copy-start = (f32[4,32,4,1024]{3,1,2,0:T(8,128)}, f32[4,32,4,1024]{3,1,2,0:T(8,128)S(1)}, u32[]{:S(2)}) copy-start(f32[4,32,4,1024]{3,1,2,0:T(8,128)S(1)} %get-tuple-element.29) | copy-start | bytes 6291460
  239.8 4.0 copy-start.5
  243.8 7.1 copy-start.15
  256.4 43.2 %all-to-all-start.3 = ((f32[64,32,256]{2,1,0:T(8,128)}), f32[64,32,256]{2,1,0:T(8,128)}, u32[]{:S(2)}, u32[]{:S(2)}) async-start(f32[64,32,256]{2,1,0:T(8,128)} %bitcast.442), calls=%async_computation.3 | async-start | bytes 4194304 | tf_op jit(solution)/shard_map/all_to_all | solution.py:139
  261.8 33.6 %collective-permute-start.2 = (f32[4,32,1,1024]{3,1,2,0:T(8,128)S(1)}, f32[4,32,1,1024]{3,1,2,0:T(8,128)S(1)}, u32[]{:S(2)}, u32[]{:S(2)}) collective-permute-start(f32[4,32,1,1024]{3,1,2,0:T(8,128)S(1)} %get-tuple-element.20), channel_id=1, source_target_pairs={{0,1},{1,2},{2,3},{3,4},{4,5},{5,6},{6,7},{8,9},{9,10},{10,11},{11... | collective-permute-start | bytes 1572872 | tf_op jit(solution)/shard_map/ppermute | solution.py:17
  266.9 43.5 %collective-permute-start.3 = (f32[4,32,1,1024]{3,1,2,0:T(8,128)}, f32[4,32,1,1024]{3,1,2,0:T(8,128)}, u32[]{:S(2)}, u32[]{:S(2)}) collective-permute-start(f32[4,32,1,1024]{3,1,2,0:T(8,128)} %get-tuple-element.19), channel_id=1, source_target_pairs={{1,0},{2,1},{3,2},{4,3},{5,4},{6,5},{7,6},{9,8},{10,9},{11,10},{12... | collective-permute-start | bytes 1572872 | tf_op jit(solution)/shard_map/ppermute | solution.py:18
  403.2 5.1 copy-start.19
  413.7 46.1 %all-to-all-start.5 = ((f32[64,32,256]{2,1,0:T(8,128)}), f32[64,32,256]{2,1,0:T(8,128)}, u32[]{:S(2)}, u32[]{:S(2)}) async-start(f32[64,32,256]{2,1,0:T(8,128)} %bitcast.441), calls=%async_computation.5 | async-start | bytes 4194304 | tf_op jit(solution)/shard_map/all_to_all | solution.py:168
  418.1 10.4 %copy-start.2 = (f32[4,32,4,1024]{3,1,2,0:T(8,128)S(1)}, f32[4,32,4,1024]{3,1,2,0:T(8,128)}, u32[]{:S(2)}) copy-start(f32[4,32,4,1024]{3,1,2,0:T(8,128)} %fusion.26) | copy-start | bytes 6291460
  420.4 35.9 %collective-permute-start.4 = (f32[4,32,1,1024]{3,1,2,0:T(8,128)S(1)}, f32[4,32,1,1024]{3,1,2,0:T(8,128)S(1)}, u32[]{:S(2)}, u32[]{:S(2)}) collective-permute-start(f32[4,32,1,1024]{3,1,2,0:T(8,128)S(1)} %get-tuple-element.18), channel_id=1, source_target_pairs={{1,0},{2,1},{3,2},{4,3},{5,4},{6,5},{7,6},{9,8},{10,9},{11,10},{12... | collective-permute-start | bytes 1572872 | tf_op jit(solution)/shard_map/ppermute | solution.py:18
  421.7 42.9 %collective-permute-start.5 = (f32[4,32,1,1024]{3,1,2,0:T(8,128)}, f32[4,32,1,1024]{3,1,2,0:T(8,128)}, u32[]{:S(2)}, u32[]{:S(2)}) collective-permute-start(f32[4,32,1,1024]{3,1,2,0:T(8,128)} %get-tuple-element.17), channel_id=1, source_target_pairs={{0,1},{1,2},{2,3},{3,4},{4,5},{5,6},{6,7},{8,9},{9,10},{10,11},{11... | collective-permute-start | bytes 1572872 | tf_op jit(solution)/shard_map/ppermute | solution.py:17
  489.6 33.0 %all-to-all-start.6 = ((f32[16,1,32768]{2,1,0:T(1,128)}), f32[16,1,32768]{2,1,0:T(1,128)}, u32[]{:S(2)}, u32[]{:S(2)}) async-start(f32[16,1,32768]{2,1,0:T(1,128)} %reshape.168), calls=%async_computation.6 | async-start | bytes 4194304 | tf_op jit(solution)/shard_map/all_to_all | solution.py:163
  494.7 207.7 %all-reduce.3.cloned.1.call-start = ((), (), s32[]{:S(2)}) async-start(), calls=%async_computation.9 | async-start | bytes 2097152
  495.0 4.2 copy-start.1
  495.0 4.2 copy-start.3
  506.0 4.2 copy-start.26
  554.5 4.1 copy-start.21
  554.5 4.1 copy-start.23
  560.7 4.7 copy-start.33
  560.7 4.7 copy-start.34
  560.8 354.3 %all-gather.3.cloned.1.call-start = ((), (), s32[]{:S(2)}) async-start(), calls=%async_computation.8 | async-start | bytes 12681216 | tf_op jit(solution)/shard_map/all_gather | solution.py:172
  566.1 4.4 copy-start.24
  578.6 168.7 %all-to-all-start.7 = ((f32[64,32,256]{2,1,0:T(8,128)}), f32[64,32,256]{2,1,0:T(8,128)}, u32[]{:S(2)}, u32[]{:S(2)}) async-start(f32[64,32,256]{2,1,0:T(8,128)} %bitcast.439), calls=%async_computation.7 | async-start | bytes 4194304 | tf_op jit(solution)/shard_map/all_to_all | solution.py:168
  584.4 50.0 %collective-permute-start.6 = (f32[4,32,1,1024]{3,1,2,0:T(8,128)}, f32[4,32,1,1024]{3,1,2,0:T(8,128)S(1)}, u32[]{:S(2)}, u32[]{:S(2)}) collective-permute-start(f32[4,32,1,1024]{3,1,2,0:T(8,128)} %get-tuple-element.16), channel_id=1, source_target_pairs={{1,0},{2,1},{3,2},{4,3},{5,4},{6,5},{7,6},{9,8},{10,9},{11,10},{12... | collective-permute-start | bytes 1572872 | tf_op jit(solution)/shard_map/ppermute | solution.py:18
  586.3 168.3 %collective-permute-start.7 = (f32[4,32,1,1024]{3,1,2,0:T(8,128)S(1)}, f32[4,32,1,1024]{3,1,2,0:T(8,128)}, u32[]{:S(2)}, u32[]{:S(2)}) collective-permute-start(f32[4,32,1,1024]{3,1,2,0:T(8,128)S(1)} %get-tuple-element.15), channel_id=1, source_target_pairs={{0,1},{1,2},{2,3},{3,4},{4,5},{5,6},{6,7},{8,9},{9,10},{10,11},{11... | collective-permute-start | bytes 1572872 | tf_op jit(solution)/shard_map/ppermute | solution.py:17
  (19 other events, 43.8 us)
Sparse Core Ops, SparseCore 0:
  560.8 141.5 all-reduce.2
Sparse Core Ops, SparseCore 1:
  566.2 348.8 all-gather.2
